TPU v7x, 256 devices: a whole 4x4x8 slice. The times are simulated.
256 devices in a mesh: tok: 8 (over x, core), hid: 32 (over y, z).
Axes of the slice: x: 4, y: 4, z: 8, core: 2. Of those that a mesh axis runs over, the one named last changes fastest.
Arguments:
- layer_input: bfloat16 [6144, 5120], P(('tok', 'hid')), may hold values from -6 to 6
- output_grad: bfloat16 [6144, 5120], P(('tok', 'hid')), may hold values from -6 to 6
- gate_weight: bfloat16 [5120, 8192], P(None, 'hid'), may hold values from -0.078125 to 0.078125
- up_weight: bfloat16 [5120, 8192], P(None, 'hid'), may hold values from -0.078125 to 0.078125
- down_weight: bfloat16 [8192, 5120], P('hid'), may hold values from -0.0625 to 0.0625
- block_lists: int32 [48, 32], P('tok'), may hold values from 0 to 63, as said below
- block_count: int32 [48], P('tok'), may hold values from 8 to 32, as said below
Outputs:
- input_grad: bfloat16 [6144, 5120], P(('tok', 'hid'))
- gate_grad: bfloat16 [5120, 8192], P('tok', 'hid')
- up_grad: bfloat16 [5120, 8192], P('tok', 'hid')
- down_grad: bfloat16 [8192, 5120], P('hid', 'tok')
Inputs may be any that keep to these rules, and one draw needn't show every extreme that they name: Each row of block_lists holds 32 different block numbers; entries past the tile's count are valid block numbers too and are not active. `block_count`: some tile uses all 32 slots and some tile uses 8.
All inputs are finite; a program needn't handle non-finite values.
Results may differ from a plain program's by a relative error of at most 0.015.
Values may be sent and summed in bfloat16 or wider, within the bound.
No kernel may reach another device: no remote copies, remote signals or barrier semaphores. Data moves between devices by JAX's collectives and lax.ppermute only.
A program may use at most 128 MiB of HBM per device.

v0:
```python
import math
import jax
import jax.numpy as jnp
from jax import lax
from jax.sharding import Mesh, PartitionSpec as P

BLOCK = 128
TILE = 128


def to_tiles(a):
    r, c = a.shape
    return a.reshape(r // 8, 8, c // 128, 128).transpose(0, 2, 1, 3).reshape(r * c // 128, 128)


def from_tiles(a, r, c):
    return a.reshape(r // 8, c // 128, 8, 128).transpose(0, 2, 1, 3).reshape(r, c)


def tile_activity(block_lists, block_count, local_blocks):
    in_list = jnp.arange(block_lists.shape[1])[None, :] < block_count[:, None]
    hits = (block_lists[:, :, None] == local_blocks[None, None, :]) & in_list[:, :, None]
    return jnp.any(hits, axis=1)


def unit_grads(gate_pre, up_pre, grad_hidden, unit_mask):
    sigmoid_g = jax.nn.sigmoid(gate_pre)
    silu_g = gate_pre * sigmoid_g
    hidden = (unit_mask * silu_g * up_pre).astype(jnp.bfloat16)
    grad_gate = (
        unit_mask * grad_hidden * up_pre * sigmoid_g * (1.0 + gate_pre * (1.0 - sigmoid_g))
    ).astype(jnp.bfloat16)
    grad_up = (unit_mask * grad_hidden * silu_g).astype(jnp.bfloat16)
    return (hidden, grad_gate, grad_up)


def body(layer_input, output_grad, gate_weight, up_weight, down_weight, block_lists, block_count):
    contract_last = (((1,), (1,)), ((), ()))
    contract_first = (((0,), (0,)), ((), ()))
    rows, d_model = layer_input.shape
    width = gate_weight.shape[1]
    blocks_here = width // BLOCK
    local_blocks = lax.axis_index("hid") * blocks_here + jnp.arange(blocks_here, dtype=jnp.int32)
    active = tile_activity(block_lists, block_count, local_blocks)
    tok_rows = rows * lax.axis_size("hid")
    inputs_full = from_tiles(
        lax.all_gather(to_tiles(layer_input), "hid", axis=0, tiled=True), tok_rows, d_model
    )
    grads_full = from_tiles(
        lax.all_gather(to_tiles(output_grad), "hid", axis=0, tiled=True), tok_rows, d_model
    )
    tiles_here = tok_rows // TILE
    unit_mask = jnp.broadcast_to(
        active.astype(jnp.float32)[:, None, :, None], (tiles_here, TILE, blocks_here, BLOCK)
    ).reshape(tok_rows, width)
    gate_pre = jnp.dot(inputs_full, gate_weight, preferred_element_type=jnp.float32)
    up_pre = jnp.dot(inputs_full, up_weight, preferred_element_type=jnp.float32)
    grad_hidden = lax.dot_general(
        grads_full, down_weight, contract_last, preferred_element_type=jnp.float32
    )
    hidden, grad_gate, grad_up = unit_grads(gate_pre, up_pre, grad_hidden, unit_mask)
    total = lax.dot_general(
        grad_gate, gate_weight, contract_last, preferred_element_type=jnp.float32
    )
    partial = (
        total
        + lax.dot_general(grad_up, up_weight, contract_last, preferred_element_type=jnp.float32)
    ).astype(jnp.bfloat16)
    input_grad = from_tiles(
        lax.psum_scatter(to_tiles(partial), "hid", scatter_dimension=0, tiled=True), rows, d_model
    )
    scale = 1.0 / math.sqrt(tok_rows * lax.axis_size("tok"))
    term_gate = lax.dot_general(
        inputs_full, grad_gate, contract_first, preferred_element_type=jnp.float32
    )
    term_up = lax.dot_general(
        inputs_full, grad_up, contract_first, preferred_element_type=jnp.float32
    )
    term_down = lax.dot_general(
        grads_full, hidden, contract_first, preferred_element_type=jnp.float32
    )
    stacked = lax.psum_scatter(
        (jnp.concatenate([term_gate, term_up, term_down], axis=1) * scale).astype(jnp.bfloat16),
        "tok",
        scatter_dimension=0,
        tiled=True,
    ).astype(jnp.float32)
    gate_grad = stacked[:, :width].astype(jnp.bfloat16)
    up_grad = stacked[:, width : 2 * width].astype(jnp.bfloat16)
    down_grad = stacked[:, 2 * width :].T.astype(jnp.bfloat16)
    return (input_grad, gate_grad, up_grad, down_grad)


def solution(mesh):
    in_specs = (
        P(("tok", "hid"), None),
        P(("tok", "hid"), None),
        P(None, "hid"),
        P(None, "hid"),
        P("hid", None),
        P("tok", None),
        P("tok"),
    )
    out_specs = (P(("tok", "hid"), None), P("tok", "hid"), P("tok", "hid"), P("hid", "tok"))
    return jax.shard_map(body, mesh=mesh, in_specs=in_specs, out_specs=out_specs, check_vma=False)
```

profile of v0, /device:TPU:2, one launch (start us, length us, event | category | flops | bytes accessed | tf_op | source)
XLA Modules:
  0.0 524.6 jit_solution(17337344538193097124)
XLA Ops:
  7.2 0.7 all-gather.5.cloned.1.call-update
  8.0 0.7 all-gather.3.cloned.1.call-update
  8.7 0.7 iota_compare_fusion
  9.5 0.9 and_reduce_fusion
  10.4 0.1 copy.15
  10.5 98.3 %all-gather.5.cloned.1.call-done = bf16[30720,128]{1,0:T(8,128)(2,1)} async-done(((bf16[960,128]{1,0:T(8,128)(2,1)}), bf16[30720,128]{1,0:T(8,128)(2,1)}) %all-gather.5.cloned.1.call-update) | async-done | bytes 7864336 | tf_op jit(solution)/shard_map/all_gather | solution.py:47
  108.8 5.6 %fusion.9 = f32[768,256]{1,0:T(8,128)S(1)} fusion(bf16[768,5120]{1,0:T(8,128)(2,1)} %bitcast.63, bf16[5120,256]{1,0:T(8,128)(2,1)S(1)} %copy-done), kind=kOutput, calls=%fused_computation.20 | convolution fusion | flops 2013265920 | bytes 11272192 | tf_op jit(solution)/shard_map/dot_general | solution.py:56
  114.4 0.7 slice-done.1
  115.1 3.1 fusion.8
  118.2 85.5 %all-gather.3.cloned.1.call-done = bf16[30720,128]{1,0:T(8,128)(2,1)} async-done(((bf16[960,128]{1,0:T(8,128)(2,1)}), bf16[30720,128]{1,0:T(8,128)(2,1)}) %all-gather.3.cloned.1.call-update) | async-done | bytes 7864336 | tf_op jit(solution)/shard_map/all_gather | solution.py:50
  203.7 0.3 broadcast_in_dim.2
  204.0 6.1 %convolution_bitcast_fusion = f32[5120,256]{0,1:T(8,128)S(1)} fusion(bf16[768,5120]{1,0:T(8,128)(2,1)} %bitcast.72, f32[768,256]{1,0:T(8,128)} %fusion.8, f32[96,8,2,128]{3,2,1,0:T(2,128)S(1)} %bitcast.76, f32[768,256]{1,0:T(8,128)S(1)} %fusion.9), kind=kOutput, calls=%fused_computation.3 | convolution fusion | flops 2014642176 | bytes 15466496 | tf_op jit(solution)/shard_map/dot_general | solution.py:79
  210.2 0.3 copy-done.5
  210.5 3.7 multiply_convert_fusion
  214.3 2.2 convolution_bitcast_fusion.1
  216.5 2.4 convolution_bitcast_fusion.2
  218.9 4.4 fusion
  223.4 10.6 %copy.18 = bf16[5120,768]{1,0:T(8,128)(2,1)} copy(bf16[5120,768]{0,1:T(8,128)(2,1)} %fusion) | data formatting | bytes 15728640
  234.1 7.7 %fusion.10 = f32[768,5120]{1,0:T(8,128)} fusion(bf16[768,256]{1,0:T(8,128)(2,1)S(1)} %get-tuple-element.17, bf16[5120,256]{1,0:T(8,128)(2,1)S(1)} %copy-done), kind=kOutput, calls=%fused_computation.21 | convolution fusion | flops 2013265920 | bytes 18743296 | tf_op jit(solution)/shard_map/dot_general | solution.py:62
  241.8 11.8 %add_convert_fusion = bf16[768,5120]{1,0:T(8,128)(2,1)} fusion(f32[768,5120]{1,0:T(8,128)} %fusion.10, bf16[768,256]{1,0:T(8,128)(2,1)S(1)} %get-tuple-element.16, bf16[5120,256]{1,0:T(8,128)(2,1)S(1)} %copy-done.2), kind=kOutput, calls=%fused_computation.2 | convolution fusion | flops 2021130240 | bytes 26607616 | tf_op jit(solution)/shard_map/dot_general | solution.py:67
  253.6 27.8 %reduce-scatter.7.cloned.1.call-done = bf16[640,768]{1,0:T(8,128)(2,1)} async-done(((bf16[5120,768]{1,0:T(8,128)(2,1)}), bf16[640,768]{1,0:T(8,128)(2,1)}) %reduce-scatter.7.cloned.1.call-update) | async-done | bytes 983056
  281.4 2.1 fusion.7
  283.5 0.9 copy.22
  284.4 233.7 %reduce-scatter.5.cloned.1.call-done = bf16[960,128]{1,0:T(8,128)(2,1)} async-done(((bf16[30720,128]{1,0:T(8,128)(2,1)}), bf16[960,128]{1,0:T(8,128)(2,1)}) %reduce-scatter.5.cloned.1.call-update) | async-done | bytes 245776 | tf_op jit(solution)/shard_map/reduce_scatter | solution.py:70
  (33 shorter events, 0.3 us)
Async XLA Ops:
  7.2 101.6 %copy-start = (bf16[5120,256]{1,0:T(8,128)(2,1)S(1)}, bf16[5120,256]{1,0:T(8,128)(2,1)}, u32[]{:S(2)}) copy-start(bf16[5120,256]{1,0:T(8,128)(2,1)} %param.9) | copy-start | bytes 7864324
  7.2 101.6 %all-gather.5.cloned.1.call-start = ((), (), s32[]{:S(2)}) async-start(), calls=%async_computation.3 | async-start | bytes 8110080 | tf_op jit(solution)/shard_map/all_gather | solution.py:47
  7.9 195.8 %all-gather.3.cloned.1.call-start = ((), (), s32[]{:S(2)}) async-start(), calls=%async_computation.2 | async-start | bytes 8110080 | tf_op jit(solution)/shard_map/all_gather | solution.py:50
  8.7 272.7 %reduce-scatter.7.cloned.1.call-start = ((), (), s32[]{:S(2)}) async-start(), calls=%async_computation.5 | async-start | bytes 8847360
  108.8 5.6 %slice-start = ((s8[7864320]{0:T(1024)(128)(4,1)}), s8[4194304]{0:T(1024)(128)(4,1)S(1)}, s32[]{:S(2)}) async-start(s8[7864320]{0:T(1024)(128)(4,1)} %bitcast.64), calls=%async_computation.6 | async-start | bytes 8388608
  108.8 5.6 %copy-start.1 = (bf16[5120,256]{1,0:T(8,128)(2,1)S(1)}, bf16[5120,256]{1,0:T(8,128)(2,1)}, u32[]{:S(2)}) copy-start(bf16[5120,256]{1,0:T(8,128)(2,1)} %param.10) | copy-start | bytes 7864324
  108.8 6.3 %slice-start.1 = ((s8[7864320]{0:T(1024)(128)(4,1)}), s8[3670016]{0:T(1024)(128)(4,1)S(1)}, s32[]{:S(2)}) async-start(s8[7864320]{0:T(1024)(128)(4,1)} %bitcast.64), calls=%async_computation.7 | async-start | bytes 7340032
  115.1 88.9 %copy-start.3 = (f32[768,256]{1,0:T(8,128)}, f32[768,256]{1,0:T(8,128)S(1)}, u32[]{:S(2)}) copy-start(f32[768,256]{1,0:T(8,128)S(1)} %fusion.9) | copy-start | bytes 2359300
  203.7 6.5 %slice-start.4 = ((s8[7864320]{0:T(1024)(128)(4,1)}), s8[4194304]{0:T(1024)(128)(4,1)S(1)}, s32[]{:S(2)}) async-start(s8[7864320]{0:T(1024)(128)(4,1)} %bitcast.73), calls=%async_computation.10 | async-start | bytes 8388608
  204.0 6.2 %slice-start.5 = ((s8[7864320]{0:T(1024)(128)(4,1)}), s8[3670016]{0:T(1024)(128)(4,1)S(1)}, s32[]{:S(2)}) async-start(s8[7864320]{0:T(1024)(128)(4,1)} %bitcast.73), calls=%async_computation.11 | async-start | bytes 7340032
  204.0 6.2 %copy-start.4 = (f32[768,256]{1,0:T(8,128)S(1)}, f32[768,256]{1,0:T(8,128)}, u32[]{:S(2)}) copy-start(f32[768,256]{1,0:T(8,128)} %fusion.8) | copy-start | bytes 2359300
  204.0 6.5 %copy-start.5 = (bf16[256,5120]{1,0:T(8,128)(2,1)S(1)}, bf16[256,5120]{1,0:T(8,128)(2,1)}, u32[]{:S(2)}) copy-start(bf16[256,5120]{1,0:T(8,128)(2,1)} %param.11) | copy-start | bytes 7864324
  204.0 10.3 %slice-start.2 = ((s8[7864320]{0:T(1024)(128)(4,1)}), s8[4194304]{0:T(1024)(128)(4,1)S(1)}, s32[]{:S(2)}) async-start(s8[7864320]{0:T(1024)(128)(4,1)} %bitcast.67), calls=%async_computation.8 | async-start | bytes 8388608
  210.5 3.8 slice-start.3
  234.0 284.0 %reduce-scatter.5.cloned.1.call-start = ((), (), s32[]{:S(2)}) async-start(), calls=%async_computation.4 | async-start | bytes 8110080 | tf_op jit(solution)/shard_map/reduce_scatter | solution.py:70
  234.1 7.7 %copy-start.2 = (bf16[5120,256]{1,0:T(8,128)(2,1)S(1)}, bf16[5120,256]{1,0:T(8,128)(2,1)}, u32[]{:S(2)}) copy-start(bf16[5120,256]{1,0:T(8,128)(2,1)} %param.10) | copy-start | bytes 7864324
Sparse Core Ops, SparseCore 0:
  10.6 98.1 all-gather.4
  111.3 92.2 all-gather.2
  234.1 47.2 reduce-scatter.6
  285.9 232.1 reduce-scatter.4
where the time goes:
time: 525 us
  waiting for transfers between devices  447 us (85%)
  matrix products  42.7 us (8%)
  local copies, waits for them, and re-layouts  15 us (3%)
  between operations  14 us (3%)
  other arithmetic  6.04 us (1%)
    reduce_scatter x1, waiting for transfers between devices, body(): lax.psum_scatter(to_tiles(partial), 'hid', scatter_dimension=0, tiled=True)  234 us
    all_gather x1, waiting for transfers between devices, body(): lax.all_gather(to_tiles(layer_input), 'hid', axis=0, tiled=True)  98.3 us
    all_gather x1, waiting for transfers between devices, body(): lax.all_gather(to_tiles(output_grad), 'hid', axis=0, tiled=True)  85.5 us
    unnamed x5, waiting for transfers between devices  29.2 us
    unnamed x26, local copies, waits for them, and re-layouts  12.6 us
    dot_general x1, matrix products, body(): lax.dot_general(grad_up, up_weight, contract_last, preferred_element_type...  11.8 us
  transfers between devices with their start and end apart: 4, of which 4 were waited for; matrix products, arithmetic and copies ran while one was open for 6% of the time, Pallas kernels for 0%

commit v1 on v0

--- a/solution.py
+++ b/solution.py
@@ -47,7 +47,12 @@
         lax.all_gather(to_tiles(layer_input), "hid", axis=0, tiled=True), tok_rows, d_model
     )
     grads_full = from_tiles(
-        lax.all_gather(to_tiles(output_grad), "hid", axis=0, tiled=True), tok_rows, d_model
+        jnp.concatenate(
+            lax.all_to_all(jnp.stack([to_tiles(output_grad)] * lax.axis_size("hid")), "hid", 0, 0),
+            axis=0,
+        ),
+        tok_rows,
+        d_model,
     )
     tiles_here = tok_rows // TILE
     unit_mask = jnp.broadcast_to(

time: 525 us -> 576 us (1.097)
  waiting for transfers between devices: 447 us -> 479 us
  starting transfers between devices: 0.16 us -> 11.9 us
    all_gather x1, waiting for transfers between devices: 98.3 us -> 212 us  [body(): lax.all_gather(to_tiles(layer_input), 'hid', axis=0, tiled=True)]
    all_gather x1 -> x0, waiting for transfers between devices: 85.5 us -> none  [body(): lax.all_gather(to_tiles(output_grad), 'hid', axis=0, tiled=True)]
    all_to_all x0 -> x1, starting transfers between devices: none -> 11.7 us  [body(): lax.all_to_all(jnp.stack([to_tiles(output_grad)] * lax.axis_size('hid')),...]
    another operation x0 -> x1, local copies, waits for them, and re-layouts: none -> 5.9 us  [body(): jnp.stack([to_tiles(output_grad)] * lax.axis_size('hid'))]
    unnamed x5 -> x4, waiting for transfers between devices: 29.2 us -> 33.5 us
  transfers between devices with their start and end apart: 4 -> 4, of which waited for: 4 -> 3; matrix products, arithmetic and copies ran while one was open for 6% -> 6% of each run, Pallas kernels for 0% -> 0%
where the time goes in v1:
time: 576 us; the launch traced here: 575 us
  waiting for transfers between devices  479 us (83%)
  matrix products  44.6 us (8%)
  local copies, waits for them, and re-layouts  20.6 us (4%)
  between operations  13.9 us (2%)
  starting transfers between devices  11.9 us (2%)
    reduce_scatter x1, waiting for transfers between devices, body(): lax.psum_scatter(to_tiles(partial), 'hid', scatter_dimension=0, tiled=True)  234 us
    all_gather x1, waiting for transfers between devices, body(): lax.all_gather(to_tiles(layer_input), 'hid', axis=0, tiled=True)  212 us
    unnamed x4, waiting for transfers between devices  33.5 us
    unnamed x26, local copies, waits for them, and re-layouts  12.2 us
    all_to_all x1, starting transfers between devices, body(): lax.all_to_all(jnp.stack([to_tiles(output_grad)] * lax.axis_size('hid')),...  11.7 us
  transfers between devices with their start and end apart: 4, of which 3 were waited for; matrix products, arithmetic and copies ran while one was open for 6% of the time, Pallas kernels for 0%

profile of v1, /device:TPU:2, one launch (start us, length us, event | category | flops | bytes accessed | tf_op | source)
XLA Modules:
  0.0 575.0 jit_solution(1236392970689320825)
XLA Ops:
  7.2 0.7 all-gather.2.cloned.1.call-update
  7.9 5.9 %stack.3 = bf16[32,960,128]{2,1,0:T(8,128)(2,1)} broadcast(bf16[960,128]{1,0:T(8,128)(2,1)} %bitcast.75), dimensions={1,2} | broadcast | bytes 8110080 | tf_op jit(solution)/shard_map/stack | solution.py:51
  13.8 11.7 %all-to-all-start = ((bf16[32,960,128]{2,1,0:T(8,128)(2,1)}), bf16[32,960,128]{2,1,0:T(8,128)(2,1)}, u32[]{:S(2)}, u32[]{:S(2)}) async-start(bf16[32,960,128]{2,1,0:T(8,128)(2,1)} %stack.3), calls=%async_computation | async-start | bytes 15728640 | tf_op jit(solution)/shard_map/all_to_all | solution.py:51
  25.6 0.0 reduce-scatter.7.cloned.1.call-start
  25.6 0.1 iota_compare_fusion
  25.7 0.2 and_reduce_fusion
  25.9 0.1 copy.15
  26.0 212.1 %all-gather.2.cloned.1.call-done = bf16[30720,128]{1,0:T(8,128)(2,1)} async-done(((bf16[960,128]{1,0:T(8,128)(2,1)}), bf16[30720,128]{1,0:T(8,128)(2,1)}) %all-gather.2.cloned.1.call-update) | async-done | bytes 7864336 | tf_op jit(solution)/shard_map/all_gather | solution.py:47
  238.1 5.6 fusion.9
  243.7 0.7 slice-done.1
  244.4 3.2 fusion.8
  247.5 0.3 broadcast_in_dim.2
  247.9 6.1 %convolution_bitcast_fusion = f32[5120,256]{0,1:T(8,128)S(1)} fusion(bf16[768,5120]{1,0:T(8,128)(2,1)} %bitcast.5, f32[768,256]{1,0:T(8,128)} %fusion.8, f32[96,8,2,128]{3,2,1,0:T(2,128)S(1)} %bitcast.72, f32[768,256]{1,0:T(8,128)S(1)} %fusion.9), kind=kOutput, calls=%fused_computation.3 | convolution fusion | flops 2014642176 | bytes 15466496 | tf_op jit(solution)/shard_map/dot_general | solution.py:84
  254.0 6.1 %multiply_convert_fusion = (bf16[768,256]{1,0:T(8,128)(2,1)S(1)}, bf16[768,256]{1,0:T(8,128)(2,1)S(1)}) fusion(f32[768,256]{1,0:T(8,128)} %copy-done.3, f32[768,256]{1,0:T(8,128)S(1)} %copy-done.4, bf16[768,5120]{1,0:T(8,128)(2,1)} %bitcast.5, bf16[256,5120]{1,0:T(8,128)(2,1)S(1)} %copy-done.6, f32[96,8,2,128]{3,2,1,0:T(2,128)S(1)} %bitcast.73), kind=kOutput, calls=%fused_computation.10 | convolution fusion | flops 2016018432 | bytes 13631488 | tf_op jit(solution)/shard_map/dot_general | solution.py:63
  260.1 2.2 convolution_bitcast_fusion.1
  262.4 2.4 convolution_bitcast_fusion.2
  264.8 4.4 fusion
  269.2 10.6 %copy.18 = bf16[5120,768]{1,0:T(8,128)(2,1)} copy(bf16[5120,768]{0,1:T(8,128)(2,1)} %fusion) | data formatting | bytes 15728640
  279.9 7.7 %fusion.10 = f32[768,5120]{1,0:T(8,128)} fusion(bf16[768,256]{1,0:T(8,128)(2,1)S(1)} %get-tuple-element.17, bf16[5120,256]{1,0:T(8,128)(2,1)S(1)} %copy-done), kind=kOutput, calls=%fused_computation.21 | convolution fusion | flops 2013265920 | bytes 18743296 | tf_op jit(solution)/shard_map/dot_general | solution.py:67
  287.7 11.2 %add_convert_fusion = bf16[768,5120]{1,0:T(8,128)(2,1)} fusion(f32[768,5120]{1,0:T(8,128)} %fusion.10, bf16[768,256]{1,0:T(8,128)(2,1)S(1)} %get-tuple-element.16, bf16[5120,256]{1,0:T(8,128)(2,1)S(1)} %copy-done.2), kind=kOutput, calls=%fused_computation.2 | convolution fusion | flops 2021130240 | bytes 26607616 | tf_op jit(solution)/shard_map/dot_general | solution.py:72
  298.9 32.7 %reduce-scatter.7.cloned.1.call-done = bf16[640,768]{1,0:T(8,128)(2,1)} async-done(((bf16[5120,768]{1,0:T(8,128)(2,1)}), bf16[640,768]{1,0:T(8,128)(2,1)}) %reduce-scatter.7.cloned.1.call-update) | async-done | bytes 983056
  331.6 2.1 fusion.7
  333.7 0.9 copy.22
  334.6 233.9 %reduce-scatter.5.cloned.1.call-done = bf16[960,128]{1,0:T(8,128)(2,1)} async-done(((bf16[30720,128]{1,0:T(8,128)(2,1)}), bf16[960,128]{1,0:T(8,128)(2,1)}) %reduce-scatter.5.cloned.1.call-update) | async-done | bytes 245776 | tf_op jit(solution)/shard_map/reduce_scatter | solution.py:75
  (32 shorter events, 0.2 us)
Async XLA Ops:
  7.2 230.9 %copy-start = (bf16[5120,256]{1,0:T(8,128)(2,1)S(1)}, bf16[5120,256]{1,0:T(8,128)(2,1)}, u32[]{:S(2)}) copy-start(bf16[5120,256]{1,0:T(8,128)(2,1)} %param.9) | copy-start | bytes 7864324
  7.2 230.9 %all-gather.2.cloned.1.call-start = ((), (), s32[]{:S(2)}) async-start(), calls=%async_computation.3 | async-start | bytes 8110080 | tf_op jit(solution)/shard_map/all_gather | solution.py:47
  13.8 11.8 %copy-start.7 = (s32[6]{0:T(128)S(1)}, s32[6]{0:T(128)}, u32[]{:S(2)}) copy-start(s32[6]{0:T(128)} %param.13) | copy-start | bytes 76
  13.8 11.9 %copy-start.5 = (s32[6,32]{1,0:T(8,128)S(1)}, s32[6,32]{1,0:T(8,128)}, u32[]{:S(2)}) copy-start(s32[6,32]{1,0:T(8,128)} %param.12) | copy-start | bytes 2308
  13.8 233.7 %all-to-all-start = ((bf16[32,960,128]{2,1,0:T(8,128)(2,1)}), bf16[32,960,128]{2,1,0:T(8,128)(2,1)}, u32[]{:S(2)}, u32[]{:S(2)}) async-start(bf16[32,960,128]{2,1,0:T(8,128)(2,1)} %stack.3), calls=%async_computation | async-start | bytes 15728640 | tf_op jit(solution)/shard_map/all_to_all | solution.py:51
  25.6 306.1 %reduce-scatter.7.cloned.1.call-start = ((), (), s32[]{:S(2)}) async-start(), calls=%async_computation.5 | async-start | bytes 8847360
  238.1 5.6 slice-start
  238.1 5.6 copy-start.1
  238.1 6.3 %slice-start.1 = ((s8[7864320]{0:T(1024)(128)(4,1)}), s8[3670016]{0:T(1024)(128)(4,1)S(1)}, s32[]{:S(2)}) async-start(s8[7864320]{0:T(1024)(128)(4,1)} %bitcast.64), calls=%async_computation.7 | async-start | bytes 7340032
  244.4 3.4 copy-start.3
  247.8 6.2 %copy-start.4 = (f32[768,256]{1,0:T(8,128)S(1)}, f32[768,256]{1,0:T(8,128)}, u32[]{:S(2)}) copy-start(f32[768,256]{1,0:T(8,128)} %fusion.8) | copy-start | bytes 2359300
  247.8 6.2 %copy-start.6 = (bf16[256,5120]{1,0:T(8,128)(2,1)S(1)}, bf16[256,5120]{1,0:T(8,128)(2,1)}, u32[]{:S(2)}) copy-start(bf16[256,5120]{1,0:T(8,128)(2,1)} %param.11) | copy-start | bytes 7864324
  247.8 12.3 %slice-start.2 = ((s8[7864320]{0:T(1024)(128)(4,1)}), s8[4194304]{0:T(1024)(128)(4,1)S(1)}, s32[]{:S(2)}) async-start(s8[7864320]{0:T(1024)(128)(4,1)} %bitcast.67), calls=%async_computation.8 | async-start | bytes 8388608
  254.0 6.1 %slice-start.3 = ((s8[7864320]{0:T(1024)(128)(4,1)}), s8[3670016]{0:T(1024)(128)(4,1)S(1)}, s32[]{:S(2)}) async-start(s8[7864320]{0:T(1024)(128)(4,1)} %bitcast.67), calls=%async_computation.9 | async-start | bytes 7340032
  279.8 288.7 %reduce-scatter.5.cloned.1.call-start = ((), (), s32[]{:S(2)}) async-start(), calls=%async_computation.4 | async-start | bytes 8110080 | tf_op jit(solution)/shard_map/reduce_scatter | solution.py:75
  279.9 7.8 %copy-start.2 = (bf16[5120,256]{1,0:T(8,128)(2,1)S(1)}, bf16[5120,256]{1,0:T(8,128)(2,1)}, u32[]{:S(2)}) copy-start(bf16[5120,256]{1,0:T(8,128)(2,1)} %param.10) | copy-start | bytes 7864324
Sparse Core Ops, SparseCore 0:
  10.6 227.4 all-gather.1
  280.0 51.6 reduce-scatter.6
  336.2 232.2 reduce-scatter.4
